TPU v7x, 32 devices: a whole 2x2x4 slice. The times are simulated.
32 devices in a mesh: chan: 4 (over y, x), facet: 8 (over z, core).
Axes of the slice: x: 2, y: 2, z: 4, core: 2. Of those that a mesh axis runs over, the one named last changes fastest.
Arguments:
- image_field: float32 [4, 2048, 2048], P('chan', 'facet'), may hold values from -6 to 6
- weights: bfloat16 [4, 2048, 2048], P('chan', None, 'facet'), may hold values from 0.049804688 to 1
- measured: bfloat16 [4, 2, 2048, 2048], P('chan', None, None, 'facet'), may hold values from -6 to 6
- dual_field: bfloat16 [4, 2, 2048, 2048], P(None, None, 'facet', 'chan'), may hold values from -3 to 3
Outputs:
- image_next: float32 [4, 2048, 2048], P(None, 'facet', 'chan')
- dual_next: bfloat16 [4, 2, 2048, 2048], P(None, None, 'facet', 'chan')
All inputs are finite; a program needn't handle non-finite values.
Results may differ from a plain program's by a relative error of at most 0.001.
Values sent between devices are 32-bit elements; how exact they have to be, the bound alone decides.
A program may use at most 128 MiB of HBM per device.

v0:
```python
from functools import partial
import math

import jax
import jax.numpy as jnp
import numpy as np
from jax import lax
from jax.experimental import pallas as pl
from jax.experimental.pallas import tpu as pltpu
from jax.sharding import PartitionSpec as P

step_primal = 0.5
step_dual = 0.5
clip_radius = 4.0
LANES = 128


def turned(real, imag, num, den, sign):
    num = num % den
    if num == 0:
        return real, imag
    if 4 * num == den:
        return (-imag, real) if sign > 0 else (imag, -real)
    c = math.cos(2.0 * math.pi * num / den)
    s = sign * math.sin(2.0 * math.pi * num / den)
    if 8 * num == den:
        h = math.sqrt(0.5)
        if sign > 0:
            return (real - imag) * h, (real + imag) * h
        return (real + imag) * h, (imag - real) * h
    return real * c - imag * s, real * s + imag * c


def block_dft(values, sign):
    n = len(values)
    if n == 1:
        return values
    even = block_dft(values[0::2], sign)
    odd = block_dft(values[1::2], sign)
    low, high = [], []
    for k in range(n // 2):
        er, ei = even[k]
        tr, ti = turned(*odd[k], k, n, sign)
        low.append((er + tr, ei + ti))
        high.append((er - tr, ei - ti))
    return low + high


def halves(x):
    high = x.astype(jnp.bfloat16)
    return high, (x - high.astype(jnp.float32)).astype(jnp.bfloat16)


def exact_dot(first, second, dims):
    (fh, fl), (sh, sl) = first, second
    dot = partial(
        lax.dot_general, dimension_numbers=(dims, ((), ())), preferred_element_type=jnp.float32
    )
    return dot(fh, sh) + (dot(fh, sl) + dot(fl, sh))


def table_seeds(blocks, inner):
    n = blocks * inner
    a = np.arange(max(blocks, inner))[:, None]
    i = np.arange(inner)[None, :]

    def pairs(step, count):
        phase = 2.0 * np.pi / n * ((step * a[:count] * i) % n)
        pair = np.stack([np.cos(phase), -np.sin(phase)], axis=1).astype(np.float32)
        pair = pair.reshape(count, 2, inner // LANES, LANES)
        return pair.transpose(0, 2, 1, 3).reshape(count, 2 * inner)

    return pairs(blocks, inner), np.repeat(pairs(1, blocks)[:, None, :], 8, axis=1)


def fill_tables(seed_ref, turn_ref, t_ref):
    _, F, A, width = t_ref.shape

    @pl.loop(0, F)
    def _(b):
        for c in range(width // (2 * LANES)):
            re_at = slice(2 * c * LANES, (2 * c + 1) * LANES)
            im_at = slice((2 * c + 1) * LANES, (2 * c + 2) * LANES)
            turn_re, turn_im = turn_ref[b, 0:1, re_at], turn_ref[b, 0:1, im_at]

            @pl.loop(0, A // 32)
            def _(t):
                rows = pl.ds(pl.multiple_of(t * 32, 32), 32)
                re, im = seed_ref[rows, re_at], seed_ref[rows, im_at]
                pair = (re * turn_re - im * turn_im, re * turn_im + im * turn_re)
                for value, at in zip(pair, (re_at, im_at)):
                    high, low = halves(value)
                    t_ref[0, b, rows, at] = high
                    t_ref[1, b, rows, at] = low


def back_pieces(rows):
    pieces, start = [], 0
    while rows - start > 32:
        size = min(LANES, (rows - start) // 2)
        pieces.append((start, size))
        start += size
    return pieces + [(start, rows - start)]


def square_tables(t_ref, k, chunks):
    found = []
    for at in (0, LANES):
        pieces = [
            [t_ref[s, k, :, 2 * LANES * c + at:2 * LANES * c + at + LANES] for c in range(chunks)]
            for s in (0, 1)
        ]
        found.append(tuple(jnp.concatenate(p, axis=1) if chunks > 1 else p[0] for p in pieces))
    return found


def halo_copy(source, target, send_sem, recv_sem, device):
    return pltpu.make_async_remote_copy(
        src_ref=source, dst_ref=target, send_sem=send_sem, recv_sem=recv_sem,
        device_id=device, device_id_type=pl.DeviceIdType.MESH,
    )


def kernel(
    F, CH, x_ref, seed_ref, turn_ref, w_hbm, m_hbm, d_hbm,
    image_hbm, grad_ref, up_hbm, left_hbm, low_ref, lowg_ref, right_ref, rightg_ref,
    t_ref, image_ref, up_ref, left_ref, dual, up, left, low, right,
    xt, z, send, recv, wb, mb, wf, mf, u, sendy, recvy, gt, g,
    in_sem, fs, fr, bs, br, cs, cr, xs, xr, ls, hs, hr, rs, rr, gs, gr,
):
    R, N = x_ref.shape
    A = N // F
    C = A // LANES
    T = N // CH
    RC = R // LANES
    W = 2 * LANES
    scale = 1.0 / N
    me = lax.axis_index("facet")
    mine = lax.axis_index("chan")
    order = sorted(range(1, F), key=lambda o: abs(o - F // 2))

    load_w = pltpu.make_async_copy(w_hbm.at[0], wb, in_sem.at[0])
    load_m = pltpu.make_async_copy(m_hbm.at[0], mb, in_sem.at[1])
    load_w.start()
    load_m.start()
    load_d = pltpu.make_async_copy(d_hbm, dual, in_sem.at[2])
    load_d.start()
    above, below = lax.rem(me + F - 1, F), lax.rem(me + 1, F)
    before, after = lax.rem(mine + CH - 1, CH), lax.rem(mine + 1, CH)

    barrier = pltpu.get_barrier_semaphore()
    for o in range(1, F):
        pl.semaphore_signal(
            barrier, inc=1, device_id={"facet": lax.rem(me + o, F)},
            device_id_type=pl.DeviceIdType.MESH,
        )
    for o in range(1, CH):
        pl.semaphore_signal(
            barrier, inc=1, device_id={"chan": lax.rem(mine + o, CH)},
            device_id_type=pl.DeviceIdType.MESH,
        )
        for f in (above, below):
            pl.semaphore_signal(
                barrier, inc=1, device_id={"chan": lax.rem(mine + o, CH), "facet": f},
                device_id_type=pl.DeviceIdType.MESH,
            )
    fill_tables(seed_ref, turn_ref, t_ref)
    load_d.wait()
    for k in range(CH):
        up[k] = dual[k, 0, R - 16:R, :].astype(jnp.float32)[8:16, :]
        left[k] = dual[k, 1, :, T - LANES:T].astype(jnp.float32)
    pl.semaphore_wait(barrier, F - 1 + 3 * (CH - 1))

    halos = [
        halo_copy(up, up_ref, hs.at[0], hr.at[0], {"facet": below}),
        halo_copy(left, left_ref, hs.at[1], hr.at[1], {"chan": after}),
    ]
    for copy in halos:
        copy.start()

    image_copies = []
    for o in range(1, CH):
        d = lax.rem(mine + o, CH)
        copy = pltpu.make_async_remote_copy(
            src_ref=x_ref.at[:, pl.ds(pl.multiple_of(d * T, LANES), T)],
            dst_ref=image_ref.at[mine],
            send_sem=xs.at[o], recv_sem=xr.at[o],
            device_id={"chan": d}, device_id_type=pl.DeviceIdType.MESH,
        )
        copy.start()
        image_copies.append(copy)
    own = pltpu.make_async_copy(
        x_ref.at[:, pl.ds(pl.multiple_of(mine * T, LANES), T)], image_ref.at[mine], ls.at[0]
    )
    own.start()
    image_copies.append(own)

    copies = []
    for c in range(C):
        wide = slice(c * W, (c + 1) * W)
        group = []
        for h in range(RC):
            if c == 0:
                for j in range(N // LANES):
                    xt[h, j * LANES:(j + 1) * LANES, :] = x_ref[
                        h * LANES:(h + 1) * LANES, j * LANES:(j + 1) * LANES
                    ].T

            @pl.loop(0, F)
            def _(b):
                part = halves(xt[h, pl.ds(b, A, stride=F), :].T)
                table = (t_ref[0, b, :, wide], t_ref[1, b, :, wide])
                z[b, 0:LANES, 0:W] = exact_dot(part, table, ((1,), (0,)))

            @pl.loop(0, LANES // 8)
            def _(t):
                rows = pl.ds(pl.multiple_of(t * 8, 8), 8)
                target = pl.ds(pl.multiple_of(h * LANES + t * 8, 8), 8)
                values = [(z[b, rows, 0:LANES], z[b, rows, LANES:W]) for b in range(F)]
                for j, (re, im) in enumerate(block_dft(values, -1.0)):
                    send[c, j, target, 0:LANES] = re
                    send[c, j, target, LANES:W] = im

            span = pl.ds(h * LANES, LANES)
            for o in order:
                d = lax.rem(me + o, F)
                copy = pltpu.make_async_remote_copy(
                    src_ref=send.at[c, d, span], dst_ref=recv.at[c, me, span],
                    send_sem=fs.at[c, h, o], recv_sem=fr.at[c, h, o],
                    device_id={"facet": d}, device_id_type=pl.DeviceIdType.MESH,
                )
                copy.start()
                group.append(copy)
            copy = pltpu.make_async_copy(
                send.at[c, me, span], recv.at[c, me, span], fr.at[c, h, 0]
            )
            copy.start()
            group.append(copy)
        copies.append(group)

    load_w.wait()
    load_m.wait()

    @pl.loop(0, N // 16)
    def _(t):
        rows = pl.ds(pl.multiple_of(t * 16, 16), 16)
        for c in range(C):
            lo = c * LANES
            wf[c, rows, :] = wb[rows, lo:lo + LANES].astype(jnp.float32) * scale
            mf[c, 0, rows, :] = mb[0, rows, lo:lo + LANES].astype(jnp.float32)
            mf[c, 1, rows, :] = mb[1, rows, lo:lo + LANES].astype(jnp.float32)

    pieces = back_pieces(R)
    back = [[] for _ in pieces]
    for c in range(C):
        wide = slice(c * W, (c + 1) * W)
        for copy in copies[c]:
            copy.wait()

        @pl.loop(0, R // 8)
        def _(t):
            rows = pl.ds(pl.multiple_of(t * 8, 8), 8)
            values = [(recv[c, q, rows, 0:LANES], recv[c, q, rows, LANES:W]) for q in range(F)]
            for k, (re, im) in enumerate(block_dft(values, -1.0)):
                u[k, rows, 0:LANES] = re
                u[k, rows, LANES:W] = im

        @pl.loop(0, F)
        def _(k):
            cos, sin = square_tables(t_ref, k, C)
            part = halves(u[k])
            p = exact_dot(cos, part, ((1,), (0,)))
            q = exact_dot(sin, part, ((1,), (0,)))
            spec_re = p[:, 0:LANES] - q[:, LANES:]
            spec_im = p[:, LANES:] + q[:, 0:LANES]
            lines = pl.ds(k, A, stride=F)
            weight = wf[c, lines, :]
            res_re = weight * spec_re - mf[c, 0, lines, :]
            res_im = weight * spec_im - mf[c, 1, lines, :]
            part = halves(jnp.concatenate([res_re, res_im], axis=1))
            p = exact_dot(cos, part, ((0,), (0,)))
            q = exact_dot(sin, part, ((0,), (0,)))
            u[k, :, 0:LANES] = p[:, 0:LANES] + q[:, LANES:]
            u[k, :, LANES:W] = p[:, LANES:] - q[:, 0:LANES]

        for i, (start, size) in enumerate(pieces if c == C - 1 else [(0, R)]):

            @pl.loop(0, size // 8)
            def _(t):
                rows = pl.ds(pl.multiple_of(start + t * 8, 8), 8)
                values = [(u[k, rows, 0:LANES], u[k, rows, LANES:W]) for k in range(F)]
                for q, (re, im) in enumerate(block_dft(values, 1.0)):
                    sendy[q, rows, c * W:c * W + LANES] = re
                    sendy[q, rows, c * W + LANES:(c + 1) * W] = im

            span = pl.ds(start, size)
            for o in order:
                d = lax.rem(me + o, F)
                copy = pltpu.make_async_remote_copy(
                    src_ref=sendy.at[d, span, wide], dst_ref=recvy.at[me, span, wide],
                    send_sem=bs.at[c, i, o], recv_sem=br.at[c, i, o],
                    device_id={"facet": d}, device_id_type=pl.DeviceIdType.MESH,
                )
                copy.start()
                back[i].append(copy)
            copy = pltpu.make_async_copy(
                sendy.at[me, span, wide], recvy.at[me, span, wide], br.at[c, i, 0]
            )
            copy.start()
            back[i].append(copy)

        if c == 0:
            for copy in image_copies + halos:
                copy.wait()
            edges = [
                pltpu.make_async_copy(image_ref, image_hbm, in_sem.at[3]),
                pltpu.make_async_copy(up_ref, up_hbm, in_sem.at[4]),
                pltpu.make_async_copy(left_ref, left_hbm, in_sem.at[5]),
            ]
            for k in range(CH):
                first_up = jnp.where(me > 0, up_ref[k], 0.0)[7:8, :]
                first_left = jnp.where(mine > 0, left_ref[k], 0.0)[:, LANES - 1:LANES]
                p = dual[k, 0, 0:16, :].astype(jnp.float32)[0:8, :]
                q = dual[k, 1, 0:16, :].astype(jnp.float32)[0:8, :]
                lane = lax.broadcasted_iota(jnp.int32, (8, T), 1)
                q_prev = jnp.where(lane == 0, first_left[0:8, :], pltpu.roll(q, 1, 1))
                low[k] = image_ref[k, 0:8, :] - (first_up - p + q_prev - q)
                p = dual[k, 0, :, 0:LANES].astype(jnp.float32)
                q = dual[k, 1, :, 0:LANES].astype(jnp.float32)
                row = lax.broadcasted_iota(jnp.int32, (R, LANES), 0)
                p_prev = jnp.where(row == 0, first_up[:, 0:LANES], pltpu.roll(p, 1, 0))
                right[k] = image_ref[k, :, 0:LANES] - (p_prev - p + first_left - q)
            edges += [
                halo_copy(low, low_ref, hs.at[2], hr.at[2], {"facet": above}),
                halo_copy(right, right_ref, hs.at[3], hr.at[3], {"chan": before}),
            ]
            for copy in edges:
                copy.start()

    last = []
    for h, (start, size) in enumerate(pieces):
        for copy in back[h]:
            copy.wait()

        @pl.loop(0, size // 8)
        def _(t):
            rows = pl.ds(pl.multiple_of(start + t * 8, 8), 8)
            target = pl.ds(pl.multiple_of(t * 8, 8), 8)
            for c in range(C):
                re_at, im_at = pl.ds(c * W, LANES), pl.ds(c * W + LANES, LANES)
                values = [(recvy[j, rows, re_at], recvy[j, rows, im_at]) for j in range(F)]
                for b, (re, im) in enumerate(block_dft(values, 1.0)):
                    z[b, target, re_at] = re
                    z[b, target, im_at] = im

        span = pl.ds(start, size)

        @pl.loop(0, F)
        def _(b):
            line = exact_dot((t_ref[0, b], t_ref[1, b]), halves(z[b]), ((1,), (1,)))
            gt[pl.ds(b, A, stride=F), :] = line * scale

        for j in range(N // LANES):
            g[span, j * LANES:(j + 1) * LANES] = gt[j * LANES:(j + 1) * LANES, :].T[0:size, :]
        if h == 0:
            for o in range(CH):
                d = lax.rem(mine + o, CH)
                copy = halo_copy(
                    g.at[0:8, pl.ds(pl.multiple_of(d * T, LANES), T)], lowg_ref.at[mine],
                    gs.at[o], gr.at[o], {"chan": d, "facet": above},
                )
                copy.start()
                last.append(copy)
        for o in range(1, CH):
            d = lax.rem(mine + o, CH)
            e = lax.rem(mine + o + 1, CH)
            copy = halo_copy(
                g.at[span, pl.ds(pl.multiple_of(e * T, LANES), LANES)],
                rightg_ref.at[mine, span], rs.at[h, o], rr.at[h, o], {"chan": d},
            )
            copy.start()
            last.append(copy)
            copy = pltpu.make_async_remote_copy(
                src_ref=g.at[span, pl.ds(pl.multiple_of(d * T, LANES), T)],
                dst_ref=grad_ref.at[mine, span],
                send_sem=cs.at[h, o], recv_sem=cr.at[h, o],
                device_id={"chan": d}, device_id_type=pl.DeviceIdType.MESH,
            )
            copy.start()
            last.append(copy)
        copy = pltpu.make_async_copy(
            g.at[span, pl.ds(pl.multiple_of(mine * T, LANES), T)],
            grad_ref.at[mine, span], ls.at[1 + h],
        )
        copy.start()
        last.append(copy)
        copy = pltpu.make_async_copy(
            g.at[span, pl.ds(pl.multiple_of(after * T, LANES), LANES)],
            rightg_ref.at[mine, span], rr.at[h, 0],
        )
        copy.start()
        last.append(copy)
    for copy in edges + last:
        copy.wait()


def gradient_tiles(F, CH, image, weights, measured, dual):
    R, N = image.shape
    A = N // F
    C = A // LANES
    RC = R // LANES
    seed, turn = (jnp.asarray(t) for t in table_seeds(F, A))
    PC = len(back_pieces(R))
    T = N // CH
    tile = jax.ShapeDtypeStruct((CH, R, T), jnp.float32)
    line = jax.ShapeDtypeStruct((CH, 8, T), jnp.float32)
    side = jax.ShapeDtypeStruct((CH, R, LANES), jnp.float32)
    f32 = jnp.float32
    dma = pltpu.SemaphoreType.DMA
    vmem = pl.BlockSpec(memory_space=pltpu.VMEM)
    hbm = pl.BlockSpec(memory_space=pl.ANY)
    return pl.pallas_call(
        partial(kernel, F, CH),
        out_shape=(tile, tile, line, side, line, line, side, side),
        in_specs=[vmem, vmem, vmem, hbm, hbm, hbm],
        out_specs=(hbm,) * 8,
        scratch_shapes=[
            pltpu.VMEM((2, F, A, 2 * A), jnp.bfloat16),
            pltpu.VMEM((CH, R, T), f32),
            pltpu.VMEM((CH, 8, T), f32),
            pltpu.VMEM((CH, R, LANES), f32),
            pltpu.VMEM((CH, 2, R, T), jnp.bfloat16),
            pltpu.VMEM((CH, 8, T), f32),
            pltpu.VMEM((CH, R, LANES), f32),
            pltpu.VMEM((CH, 8, T), f32),
            pltpu.VMEM((CH, R, LANES), f32),
            pltpu.VMEM((RC, N, LANES), f32),
            pltpu.VMEM((F, LANES, 2 * A), f32),
            pltpu.VMEM((C, F, R, 2 * LANES), f32),
            pltpu.VMEM((C, F, R, 2 * LANES), f32),
            pltpu.VMEM((N, A), jnp.bfloat16),
            pltpu.VMEM((2, N, A), jnp.bfloat16),
            pltpu.VMEM((C, N, LANES), f32),
            pltpu.VMEM((C, 2, N, LANES), f32),
            pltpu.VMEM((F, A, 2 * LANES), f32),
            pltpu.VMEM((F, R, 2 * A), f32),
            pltpu.VMEM((F, R, 2 * A), f32),
            pltpu.VMEM((N, LANES), f32),
            pltpu.VMEM((R, N), f32),
            dma((6,)),
            dma((C, RC, F)), dma((C, RC, F)),
            dma((C, PC, F)), dma((C, PC, F)),
            dma((PC, CH)), dma((PC, CH)),
            dma((CH,)), dma((CH,)),
            dma((1 + PC,)),
            dma((4,)), dma((4,)),
            dma((PC, CH)), dma((PC, CH)),
            dma((CH,)), dma((CH,)),
        ],
        compiler_params=pltpu.CompilerParams(
            collective_id=0, has_side_effects=True, vmem_limit_bytes=60 * 1024 * 1024
        ),
    )(image, seed, turn, weights, measured, dual)


def prior_kernel(
    n, edge, x, g, d, up, left, low, lowg, right, rightg, image, dual, ext, held, carry, parts
):
    t = pl.program_id(0)
    CH, TR, T = x.shape
    now = lax.rem(t, 2)
    row = lax.broadcasted_iota(jnp.int32, (TR, T), 0)
    lane = lax.broadcasted_iota(jnp.int32, (TR, T), 1)

    @pl.when(t == 0)
    def _():
        carry[...] = jnp.where(edge[0] == 0, 0.0, up[...])

    @pl.when(t < n)
    def _():
        for c in range(CH):
            p = d[c, 0].astype(jnp.float32)
            q = d[c, 1].astype(jnp.float32)
            p_prev = jnp.where(row == 0, carry[c, 7:8, :], pltpu.roll(p, 1, 0))
            first = jnp.where(edge[2] == 0, 0.0, left[c])[:, LANES - 1:LANES]
            q_prev = jnp.where(lane == 0, first, pltpu.roll(q, 1, 1))
            adjoint = p_prev - p + q_prev - q
            value = x[c] - step_primal * (g[c] + adjoint)
            image[c] = value
            ext[now, c] = 2.0 * value - x[c]
            held[now, c, 0] = p
            held[now, c, 1] = q
            carry[c] = p[TR - 8:TR, :]

    @pl.when(t > 0)
    def _():
        was = 1 - now
        total = jnp.zeros((TR, T), jnp.float32)
        for c in range(CH):
            e = ext[was, c]
            beyond = jnp.where(edge[1] == 0, 0.0, low[c] - lowg[c])
            following = jnp.where(t < n, ext[now, c, 0:8, :], beyond)[0:1, :]
            rows = jnp.where(row == TR - 1, following, pltpu.roll(e, TR - 1, 0)) - e
            side = jnp.where(edge[3] == 0, 0.0, right[c] - rightg[c])[:, 0:1]
            cols = jnp.where(lane == T - 1, side, pltpu.roll(e, T - 1, 1)) - e
            first_part = held[was, c, 0] + step_dual * rows
            second_part = held[was, c, 1] + step_dual * cols
            parts[c, 0] = first_part
            parts[c, 1] = second_part
            total = total + (first_part * first_part + second_part * second_part)
        factor = 1.0 / jnp.maximum(1.0, jnp.sqrt(total) / clip_radius)
        for c in range(CH):
            dual[c, 0] = (parts[c, 0] * factor).astype(jnp.bfloat16)
            dual[c, 1] = (parts[c, 1] * factor).astype(jnp.bfloat16)


def prior(edge, x, g, dual, up, left, low, lowg, right, rightg):
    CH, R, T = x.shape
    TR = 64
    n = R // TR
    f32 = jnp.float32
    ahead = lambda t: jnp.minimum(t, n - 1)
    behind = lambda t: jnp.maximum(t - 1, 0)
    tile = pl.BlockSpec((CH, TR, T), lambda t: (0, ahead(t), 0))
    line = pl.BlockSpec((CH, 8, T), lambda t: (0, 0, 0))
    return pl.pallas_call(
        partial(prior_kernel, n),
        grid=(n + 1,),
        out_shape=(
            jax.ShapeDtypeStruct((CH, R, T), f32),
            jax.ShapeDtypeStruct((CH, 2, R, T), jnp.bfloat16),
        ),
        in_specs=[
            pl.BlockSpec(memory_space=pltpu.SMEM),
            tile,
            tile,
            pl.BlockSpec((CH, 2, TR, T), lambda t: (0, 0, ahead(t), 0)),
            line,
            pl.BlockSpec((CH, TR, LANES), lambda t: (0, ahead(t), 0)),
            line,
            line,
            pl.BlockSpec((CH, TR, LANES), lambda t: (0, behind(t), 0)),
            pl.BlockSpec((CH, TR, LANES), lambda t: (0, behind(t), 0)),
        ],
        out_specs=(tile, pl.BlockSpec((CH, 2, TR, T), lambda t: (0, 0, behind(t), 0))),
        scratch_shapes=[
            pltpu.VMEM((2, CH, TR, T), f32),
            pltpu.VMEM((2, CH, 2, TR, T), f32),
            pltpu.VMEM((CH, 8, T), f32),
            pltpu.VMEM((CH, 2, TR, T), f32),
        ],
        compiler_params=pltpu.CompilerParams(vmem_limit_bytes=60 * 1024 * 1024),
    )(edge, x, g, dual, up, left, low, lowg, right, rightg)


def shards(image_field, weights, measured, dual_field):
    F, CH = lax.axis_size("facet"), lax.axis_size("chan")
    tiles = gradient_tiles(F, CH, image_field[0], weights, measured, dual_field)
    f, c = lax.axis_index("facet"), lax.axis_index("chan")
    edge = jnp.stack([f > 0, f < F - 1, c > 0, c < CH - 1]).astype(jnp.int32)
    return prior(edge, tiles[0], tiles[1], dual_field, *tiles[2:])


def solution(mesh):
    placed = (
        P("chan", "facet", None),
        P("chan", None, "facet"),
        P("chan", None, None, "facet"),
        P(None, None, "facet", "chan"),
    )
    return jax.shard_map(
        shards,
        mesh=mesh,
        in_specs=placed,
        out_specs=(P(None, "facet", "chan"), P(None, None, "facet", "chan")),
        check_vma=False,
    )
```

profile of v0, /device:TPU:9, one launch (start us, length us, event | category | flops | bytes accessed | tf_op | source)
XLA Modules:
  0.0 224.4 jit_solution(1568974513401581892)
XLA Ops:
  0.6 0.6 add_convert_fusion.edge
  1.2 216.1 %shard_map.77 = (f32[4,256,512]{2,1,0:T(8,128)}, f32[4,256,512]{2,1,0:T(8,128)}, f32[4,8,512]{2,1,0:T(8,128)}, f32[4,256,128]{2,1,0:T(8,128)}, f32[4,8,512]{2,1,...) custom-call(f32[256,2048]{1,0:T(8,128)} %bitcast.5, ...), custom_call_target="tpu_custom_call" | custom-call | tf_op jit(solution)/shard_map/pallas_call | solution.py:422
  217.3 7.0 %shard_map.78 = (f32[4,256,512]{2,1,0:T(8,128)}, bf16[4,2,256,512]{3,2,1,0:T(8,128)(2,1)}) custom-call(s32[4]{0:T(128)} %add_convert_fusion.edge, f32[4,256,512]{2,1,0:T(8,128)} %get-tuple-element.10.x, f32[4,256,512]{2,1,0:T(8,128)} %get-tuple-element.11.g, bf16[4,2,256,512]{3,2,1,0:T(8,128)(2,1)} %d.1, f32[4,8,512]{2,1,0:T(8,128)} %get-tuple-element.12.up, ...), custom_call_target="tpu_custom_call" | custom-call | tf_op jit(solution)/shard_map/pallas_call | solution.py:526
where the time goes:
time: 225 us; the launch traced here: 224 us
  Pallas kernels  223 us (99%)
    pallas_call x1, Pallas kernels, gradient_tiles(): pl.pallas_call(partial(kernel, F, CH), out_shape=(tile, tile, line, side,...  216 us
    pallas_call x1, Pallas kernels, prior(): pl.pallas_call(partial(prior_kernel, n), grid=(n + 1,), out_shape=(jax.Sh...  7.02 us

commit v1 on v0

v1 whole, which is shorter than its diff:
```python
from functools import partial
import math

import jax
import jax.numpy as jnp
import numpy as np
from jax import lax
from jax.experimental import pallas as pl
from jax.experimental.pallas import tpu as pltpu
from jax.sharding import PartitionSpec as P

step_primal = 0.5
step_dual = 0.5
clip_radius = 4.0
LANES = 128
BLOCK = 16


def turned(real, imag, num, den, sign):
    num = num % den
    if num == 0:
        return real, imag
    if 4 * num == den:
        return (-imag, real) if sign > 0 else (imag, -real)
    c = math.cos(2.0 * math.pi * num / den)
    s = sign * math.sin(2.0 * math.pi * num / den)
    if 8 * num == den:
        h = math.sqrt(0.5)
        if sign > 0:
            return (real - imag) * h, (real + imag) * h
        return (real + imag) * h, (imag - real) * h
    return real * c - imag * s, real * s + imag * c


def block_dft(values, sign):
    n = len(values)
    if n == 1:
        return values
    even = block_dft(values[0::2], sign)
    odd = block_dft(values[1::2], sign)
    low, high = [], []
    for k in range(n // 2):
        er, ei = even[k]
        tr, ti = turned(*odd[k], k, n, sign)
        low.append((er + tr, ei + ti))
        high.append((er - tr, ei - ti))
    return low + high


def halves(x):
    high = x.astype(jnp.bfloat16)
    return high, (x - high.astype(jnp.float32)).astype(jnp.bfloat16)


def exact_dot(first, second, dims):
    (fh, fl), (sh, sl) = first, second
    dot = partial(
        lax.dot_general, dimension_numbers=(dims, ((), ())), preferred_element_type=jnp.float32
    )
    return dot(fh, sh) + (dot(fh, sl) + dot(fl, sh))


def table_seeds(blocks, inner):
    n = blocks * inner
    a = np.arange(max(blocks, inner))[:, None]
    i = np.arange(inner)[None, :]

    def pairs(step, count):
        phase = 2.0 * np.pi / n * ((step * a[:count] * i) % n)
        pair = np.stack([np.cos(phase), -np.sin(phase)], axis=1).astype(np.float32)
        pair = pair.reshape(count, 2, inner // LANES, LANES)
        return pair.transpose(0, 2, 1, 3).reshape(count, 2 * inner)

    phase = 2.0 * np.pi / n * ((blocks * a[None, :inner] + a[:blocks, None]) * i[:, :LANES] % n)
    value = np.concatenate([np.cos(phase), -np.sin(phase)], axis=2).astype(np.float32)
    high = value.astype(jnp.bfloat16)
    low = (value - high.astype(np.float32)).astype(jnp.bfloat16)
    return pairs(blocks, inner), np.repeat(pairs(1, blocks)[:, None, :], 8, axis=1), np.stack([high, low])


def fill_tables(seed_ref, turn_ref, t_ref):
    _, F, A, width = t_ref.shape

    @pl.loop(0, F)
    def _(b):
        for c in range(1, width // (2 * LANES)):
            re_at = slice(2 * c * LANES, (2 * c + 1) * LANES)
            im_at = slice((2 * c + 1) * LANES, (2 * c + 2) * LANES)
            turn_re, turn_im = turn_ref[b, 0:1, re_at], turn_ref[b, 0:1, im_at]

            @pl.loop(0, A // 32)
            def _(t):
                rows = pl.ds(pl.multiple_of(t * 32, 32), 32)
                re, im = seed_ref[rows, re_at], seed_ref[rows, im_at]
                pair = (re * turn_re - im * turn_im, re * turn_im + im * turn_re)
                for value, at in zip(pair, (re_at, im_at)):
                    high, low = halves(value)
                    t_ref[0, b, rows, at] = high
                    t_ref[1, b, rows, at] = low


def back_pieces(rows):
    pieces, start = [], 0
    for part in (4, 4, 4, 8, 8):
        pieces.append((start, rows // part))
        start += rows // part
    return pieces


def square_tables(t_ref, k, chunks):
    found = []
    for at in (0, LANES):
        pieces = [
            [t_ref[s, k, :, 2 * LANES * c + at:2 * LANES * c + at + LANES] for c in range(chunks)]
            for s in (0, 1)
        ]
        found.append(tuple(jnp.concatenate(p, axis=1) if chunks > 1 else p[0] for p in pieces))
    return found


def halo_copy(source, target, send_sem, recv_sem, device):
    return pltpu.make_async_remote_copy(
        src_ref=source, dst_ref=target, send_sem=send_sem, recv_sem=recv_sem,
        device_id=device, device_id_type=pl.DeviceIdType.MESH,
    )


def kernel(
    F, CH, x_hbm, seed_ref, turn_ref, table_hbm, w_hbm, m_hbm, d_hbm,
    image_hbm, next_hbm,
    t_ref, x_ref, image_ref, grad_ref, dual, up, up_ref, low, low_ref,
    left, left_ref, right, right_ref, edge, edge_ref, column, parts,
    xt, z, send, recv, wb, mb, wf, mf, u, sendy, recvy, gt, g,
    in_sem, fs, fr, bs, br, cs, cr, xs, xr, ls, hs, hr, rs, rr, out_sem,
):
    R, N = x_ref.shape
    A = N // F
    C = A // LANES
    T = N // CH
    RC = R // LANES
    W = 2 * LANES
    scale = 1.0 / N
    me = lax.axis_index("facet")
    mine = lax.axis_index("chan")
    order = sorted(range(1, F), key=lambda o: abs(o - F // 2))

    load_x = [
        pltpu.make_async_copy(
            x_hbm.at[h * LANES:(h + 1) * LANES], x_ref.at[h * LANES:(h + 1) * LANES],
            in_sem.at[6 + h],
        )
        for h in range(RC)
    ]
    load_t = pltpu.make_async_copy(table_hbm, t_ref.at[:, :, :, 0:W], in_sem.at[6 + RC])
    load_x[0].start()
    load_t.start()
    for copy in load_x[1:]:
        copy.start()
    load_w = pltpu.make_async_copy(w_hbm.at[0], wb, in_sem.at[0])
    load_m = pltpu.make_async_copy(m_hbm.at[0], mb, in_sem.at[1])
    load_w.start()
    load_m.start()
    load_d = pltpu.make_async_copy(d_hbm, dual, in_sem.at[2])
    load_d.start()
    above, below = lax.rem(me + F - 1, F), lax.rem(me + 1, F)
    before, after = lax.rem(mine + CH - 1, CH), lax.rem(mine + 1, CH)

    barrier = pltpu.get_barrier_semaphore()
    for o in range(1, F):
        pl.semaphore_signal(
            barrier, inc=1, device_id={"facet": lax.rem(me + o, F)},
            device_id_type=pl.DeviceIdType.MESH,
        )
    for o in range(1, CH):
        pl.semaphore_signal(
            barrier, inc=1, device_id={"chan": lax.rem(mine + o, CH)},
            device_id_type=pl.DeviceIdType.MESH,
        )

    copies = []
    for c in range(C):
        wide = slice(c * W, (c + 1) * W)
        group = []
        for h in range(RC):
            if c == 0:
                load_x[h].wait()
                for j in range(N // LANES):
                    xt[h, j * LANES:(j + 1) * LANES, :] = x_ref[
                        h * LANES:(h + 1) * LANES, j * LANES:(j + 1) * LANES
                    ].T

            if c == 0 and h == 0:
                load_t.wait()

            @pl.loop(0, F)
            def _(b):
                part = halves(xt[h, pl.ds(b, A, stride=F), :].T)
                table = (t_ref[0, b, :, wide], t_ref[1, b, :, wide])
                z[b, 0:LANES, 0:W] = exact_dot(part, table, ((1,), (0,)))

            @pl.loop(0, LANES // 8)
            def _(t):
                rows = pl.ds(pl.multiple_of(t * 8, 8), 8)
                target = pl.ds(pl.multiple_of(h * LANES + t * 8, 8), 8)
                values = [(z[b, rows, 0:LANES], z[b, rows, LANES:W]) for b in range(F)]
                for j, (re, im) in enumerate(block_dft(values, -1.0)):
                    send[c, j, target, 0:LANES] = re
                    send[c, j, target, LANES:W] = im

            if c == 0 and h == 0:
                pl.semaphore_wait(barrier, F - 1 + CH - 1)
            span = pl.ds(h * LANES, LANES)
            for o in order:
                d = lax.rem(me + o, F)
                copy = pltpu.make_async_remote_copy(
                    src_ref=send.at[c, d, span], dst_ref=recv.at[c, me, span],
                    send_sem=fs.at[c, h, o], recv_sem=fr.at[c, h, o],
                    device_id={"facet": d}, device_id_type=pl.DeviceIdType.MESH,
                )
                copy.start()
                group.append(copy)
            copy = pltpu.make_async_copy(
                send.at[c, me, span], recv.at[c, me, span], fr.at[c, h, 0]
            )
            copy.start()
            group.append(copy)
        copies.append(group)
        if c == 0:
            fill_tables(seed_ref, turn_ref, t_ref)
            load_d.wait()
            for k in range(CH):
                up[k:k + 1, :] = dual[k, 0, R - 16:R, :].astype(jnp.float32)[15:16, :]
                left[k] = dual[k, 1, :, T - LANES:T].astype(jnp.float32)
            halos = [
                halo_copy(up, up_ref, hs.at[0], hr.at[0], {"facet": below}),
                halo_copy(left, left_ref, hs.at[1], hr.at[1], {"chan": after}),
            ]
            for copy in halos:
                copy.start()

            image_copies = []
            for o in range(1, CH):
                d = lax.rem(mine + o, CH)
                copy = pltpu.make_async_remote_copy(
                    src_ref=x_ref.at[:, pl.ds(pl.multiple_of(d * T, LANES), T)],
                    dst_ref=image_ref.at[mine, 0:R],
                    send_sem=xs.at[o], recv_sem=xr.at[o],
                    device_id={"chan": d}, device_id_type=pl.DeviceIdType.MESH,
                )
                copy.start()
                image_copies.append(copy)
            own = pltpu.make_async_copy(
                x_ref.at[:, pl.ds(pl.multiple_of(mine * T, LANES), T)], image_ref.at[mine, 0:R], ls.at[0]
            )
            own.start()
            image_copies.append(own)

    load_w.wait()
    load_m.wait()

    @pl.loop(0, N // 16)
    def _(t):
        rows = pl.ds(pl.multiple_of(t * 16, 16), 16)
        for c in range(C):
            lo = c * LANES
            wf[c, rows, :] = wb[rows, lo:lo + LANES].astype(jnp.float32) * scale
            mf[c, 0, rows, :] = mb[0, rows, lo:lo + LANES].astype(jnp.float32)
            mf[c, 1, rows, :] = mb[1, rows, lo:lo + LANES].astype(jnp.float32)

    pieces = back_pieces(R)
    back = [[] for _ in pieces]
    for c in range(C):
        wide = slice(c * W, (c + 1) * W)
        for copy in copies[c]:
            copy.wait()

        @pl.loop(0, R // 8)
        def _(t):
            rows = pl.ds(pl.multiple_of(t * 8, 8), 8)
            values = [(recv[c, q, rows, 0:LANES], recv[c, q, rows, LANES:W]) for q in range(F)]
            for k, (re, im) in enumerate(block_dft(values, -1.0)):
                u[k, rows, 0:LANES] = re
                u[k, rows, LANES:W] = im

        @pl.loop(0, F)
        def _(k):
            cos, sin = square_tables(t_ref, k, C)
            part = halves(u[k])
            p = exact_dot(cos, part, ((1,), (0,)))
            q = exact_dot(sin, part, ((1,), (0,)))
            spec_re = p[:, 0:LANES] - q[:, LANES:]
            spec_im = p[:, LANES:] + q[:, 0:LANES]
            lines = pl.ds(k, A, stride=F)
            weight = wf[c, lines, :]
            res_re = weight * spec_re - mf[c, 0, lines, :]
            res_im = weight * spec_im - mf[c, 1, lines, :]
            part = halves(jnp.concatenate([res_re, res_im], axis=1))
            p = exact_dot(cos, part, ((0,), (0,)))
            q = exact_dot(sin, part, ((0,), (0,)))
            u[k, :, 0:LANES] = p[:, 0:LANES] + q[:, LANES:]
            u[k, :, LANES:W] = p[:, LANES:] - q[:, 0:LANES]

        for i, (start, size) in enumerate(pieces if c == C - 1 else [(0, R)]):

            @pl.loop(0, size // 8)
            def _(t):
                rows = pl.ds(pl.multiple_of(start + t * 8, 8), 8)
                values = [(u[k, rows, 0:LANES], u[k, rows, LANES:W]) for k in range(F)]
                for q, (re, im) in enumerate(block_dft(values, 1.0)):
                    sendy[q, rows, c * W:c * W + LANES] = re
                    sendy[q, rows, c * W + LANES:(c + 1) * W] = im

            span = pl.ds(start, size)
            for o in order:
                d = lax.rem(me + o, F)
                copy = pltpu.make_async_remote_copy(
                    src_ref=sendy.at[d, span, wide], dst_ref=recvy.at[me, span, wide],
                    send_sem=bs.at[c, i, o], recv_sem=br.at[c, i, o],
                    device_id={"facet": d}, device_id_type=pl.DeviceIdType.MESH,
                )
                copy.start()
                back[i].append(copy)
            copy = pltpu.make_async_copy(
                sendy.at[me, span, wide], recvy.at[me, span, wide], br.at[c, i, 0]
            )
            copy.start()
            back[i].append(copy)

        if c == 0:
            for copy in image_copies + halos:
                copy.wait()
            for k in range(CH):
                first_up = jnp.where(me > 0, up_ref[k:k + 1, 0:LANES], 0.0)
                first_left = jnp.where(mine > 0, left_ref[k], 0.0)[:, LANES - 1:LANES]
                p = dual[k, 0, :, 0:LANES].astype(jnp.float32)
                q = dual[k, 1, :, 0:LANES].astype(jnp.float32)
                row = lax.broadcasted_iota(jnp.int32, (R, LANES), 0)
                p_prev = jnp.where(row == 0, first_up, pltpu.roll(p, 1, 0))
                right[k] = image_ref[k, 0:R, 0:LANES] - (p_prev - p + first_left - q)
            edges = [halo_copy(right, right_ref, hs.at[3], hr.at[3], {"chan": before})]
            for copy in edges:
                copy.start()

    row = lax.broadcasted_iota(jnp.int32, (BLOCK, T), 0)
    lane = lax.broadcasted_iota(jnp.int32, (BLOCK, T), 1)

    def primal(first, end):
        @pl.loop(first, end)
        def _(at):
            rows = pl.ds(pl.multiple_of(at * BLOCK, BLOCK), BLOCK)
            ahead = pl.ds(pl.multiple_of(jnp.maximum(at - 1, 0) * BLOCK, BLOCK), BLOCK)
            for k in range(CH):
                p = dual[k, 0, rows, :].astype(jnp.float32)
                q = dual[k, 1, rows, :].astype(jnp.float32)
                top = dual[k, 0, ahead, :].astype(jnp.float32)[BLOCK - 1:BLOCK, :]
                top = jnp.where(at > 0, top, jnp.where(me > 0, up_ref[k:k + 1, :], 0.0))
                p_prev = jnp.where(row == 0, top, pltpu.roll(p, 1, 0))
                start = jnp.where(mine > 0, left_ref[k, rows, :], 0.0)[:, LANES - 1:LANES]
                q_prev = jnp.where(lane == 0, start, pltpu.roll(q, 1, 1))
                adjoint = p_prev - p + q_prev - q
                x = image_ref[k, rows, :]
                value = x - step_primal * (grad_ref[k, rows, :] + adjoint)
                grad_ref[k, rows, :] = value
                image_ref[k, rows, :] = 2.0 * value - x

    def shrink(first, end):
        @pl.loop(first, end)
        def _(at):
            rows = pl.ds(pl.multiple_of(at * BLOCK, BLOCK), BLOCK)
            later = pl.ds(pl.multiple_of(at * BLOCK + BLOCK, BLOCK), 8)
            total = jnp.zeros((BLOCK, T), jnp.float32)
            for k in range(CH):
                e = image_ref[k, rows, :]
                following = image_ref[k, later, :][0:1, :]
                down = jnp.where(row == BLOCK - 1, following, pltpu.roll(e, BLOCK - 1, 0)) - e
                side = right_ref[k, rows, :][:, 0:1] - column[rows, :][:, k:k + 1]
                side = jnp.where(mine < CH - 1, side, 0.0)
                over = jnp.where(lane == T - 1, side, pltpu.roll(e, T - 1, 1)) - e
                first_part = dual[k, 0, rows, :].astype(jnp.float32) + step_dual * down
                second_part = dual[k, 1, rows, :].astype(jnp.float32) + step_dual * over
                parts[k, 0] = first_part
                parts[k, 1] = second_part
                total = total + (first_part * first_part + second_part * second_part)
            factor = 1.0 / jnp.maximum(1.0, jnp.sqrt(total) / clip_radius)
            for k in range(CH):
                dual[k, 0, rows, :] = (parts[k, 0] * factor).astype(jnp.bfloat16)
                dual[k, 1, rows, :] = (parts[k, 1] * factor).astype(jnp.bfloat16)

    last = [[] for _ in pieces]
    outs = []

    def finish(h):
        start, size = pieces[h]
        for copy in last[h]:
            copy.wait()
        if h == 0:
            for copy in edges:
                copy.wait()
        tile = jnp.concatenate([edge_ref[k, h, 0:1, :] for k in range(CH)], axis=0)
        tile = jnp.concatenate([tile] * (LANES // CH), axis=0)
        column[start:start + size, :] = tile.T[0:size, :]
        primal(start // BLOCK, (start + size) // BLOCK)
        if h == 0:
            for k in range(CH):
                low[k:k + 1, :] = image_ref[k, 0:8, :][0:1, :]
            copy = halo_copy(low, low_ref, hs.at[2], hr.at[2], {"facet": above})
            copy.start()
            edges.append(copy)
        final = h == len(pieces) - 1
        if final:
            edges[-1].wait()
            for k in range(CH):
                image_ref[k, R:R + 1, :] = jnp.where(me < F - 1, low_ref[k:k + 1, :], 0.0)
        first = max(start // BLOCK - 1, 0)
        end = (start + size) // BLOCK - (0 if final else 1)
        shrink(first, end)
        done = slice(start, start + size)
        outs.append(pltpu.make_async_copy(
            grad_ref.at[:, done, :], image_hbm.at[:, done, :], out_sem.at[0, h]
        ))
        done = slice(first * BLOCK, end * BLOCK)
        outs.append(pltpu.make_async_copy(
            dual.at[:, :, done, :], next_hbm.at[:, :, done, :], out_sem.at[1, h]
        ))
        for copy in outs[-2:]:
            copy.start()

    for h, (start, size) in enumerate(pieces):
        for copy in back[h]:
            copy.wait()

        @pl.loop(0, size // 8)
        def _(t):
            rows = pl.ds(pl.multiple_of(start + t * 8, 8), 8)
            target = pl.ds(pl.multiple_of(t * 8, 8), 8)
            for c in range(C):
                re_at, im_at = pl.ds(c * W, LANES), pl.ds(c * W + LANES, LANES)
                values = [(recvy[j, rows, re_at], recvy[j, rows, im_at]) for j in range(F)]
                for b, (re, im) in enumerate(block_dft(values, 1.0)):
                    z[b, target, re_at] = re
                    z[b, target, im_at] = im

        span = pl.ds(start, size)

        @pl.loop(0, F)
        def _(b):
            line = exact_dot((t_ref[0, b], t_ref[1, b]), halves(z[b]), ((1,), (1,)))
            gt[pl.ds(b, A, stride=F), :] = line * scale

        for e in range(CH):
            edge[h, e] = gt[e * T:e * T + 8, :]
        for j in range(N // LANES):
            g[span, j * LANES:(j + 1) * LANES] = gt[j * LANES:(j + 1) * LANES, :].T[0:size, :]
        for o in range(1, CH):
            d = lax.rem(mine + o, CH)
            last[h].append(pltpu.make_async_remote_copy(
                src_ref=g.at[span, pl.ds(pl.multiple_of(d * T, LANES), T)],
                dst_ref=grad_ref.at[mine, span],
                send_sem=cs.at[h, o], recv_sem=cr.at[h, o],
                device_id={"chan": d}, device_id_type=pl.DeviceIdType.MESH,
            ))
            last[h].append(halo_copy(
                edge.at[h, lax.rem(mine + o + 1, CH)], edge_ref.at[mine, h],
                rs.at[h, o], rr.at[h, o], {"chan": d},
            ))
        last[h].append(pltpu.make_async_copy(
            g.at[span, pl.ds(pl.multiple_of(mine * T, LANES), T)],
            grad_ref.at[mine, span], ls.at[1 + h],
        ))
        last[h].append(pltpu.make_async_copy(
            edge.at[h, after], edge_ref.at[mine, h], rr.at[h, 0]
        ))
        for copy in last[h]:
            copy.start()
        if h > 0:
            finish(h - 1)
    finish(len(pieces) - 1)
    for copy in outs:
        copy.wait()


def shards(image, weights, measured, dual):
    F, CH = lax.axis_size("facet"), lax.axis_size("chan")
    R, N = image.shape[1:]
    A = N // F
    C = A // LANES
    RC = R // LANES
    seed, turn, table = (jnp.asarray(t) for t in table_seeds(F, A))
    PC = len(back_pieces(R))
    T = N // CH
    HR = -(-CH // 8) * 8
    f32 = jnp.float32
    dma = pltpu.SemaphoreType.DMA
    vmem = pl.BlockSpec(memory_space=pltpu.VMEM)
    hbm = pl.BlockSpec(memory_space=pl.ANY)
    return pl.pallas_call(
        partial(kernel, F, CH),
        out_shape=(
            jax.ShapeDtypeStruct((CH, R, T), f32),
            jax.ShapeDtypeStruct((CH, 2, R, T), jnp.bfloat16),
        ),
        in_specs=[hbm, vmem, vmem, hbm, hbm, hbm, hbm],
        out_specs=(hbm, hbm),
        scratch_shapes=[
            pltpu.VMEM((2, F, A, 2 * A), jnp.bfloat16),
            pltpu.VMEM((R, N), f32),
            pltpu.VMEM((CH, R + 8, T), f32),
            pltpu.VMEM((CH, R, T), f32),
            pltpu.VMEM((CH, 2, R, T), jnp.bfloat16),
            pltpu.VMEM((HR, T), f32),
            pltpu.VMEM((HR, T), f32),
            pltpu.VMEM((HR, T), f32),
            pltpu.VMEM((HR, T), f32),
            pltpu.VMEM((CH, R, LANES), f32),
            pltpu.VMEM((CH, R, LANES), f32),
            pltpu.VMEM((CH, R, LANES), f32),
            pltpu.VMEM((CH, R, LANES), f32),
            pltpu.VMEM((PC, CH, 8, LANES), f32),
            pltpu.VMEM((CH, PC, 8, LANES), f32),
            pltpu.VMEM((R, LANES), f32),
            pltpu.VMEM((CH, 2, BLOCK, T), f32),
            pltpu.VMEM((RC, N, LANES), f32),
            pltpu.VMEM((F, LANES, 2 * A), f32),
            pltpu.VMEM((C, F, R, 2 * LANES), f32),
            pltpu.VMEM((C, F, R, 2 * LANES), f32),
            pltpu.VMEM((N, A), jnp.bfloat16),
            pltpu.VMEM((2, N, A), jnp.bfloat16),
            pltpu.VMEM((C, N, LANES), f32),
            pltpu.VMEM((C, 2, N, LANES), f32),
            pltpu.VMEM((F, A, 2 * LANES), f32),
            pltpu.VMEM((F, R, 2 * A), f32),
            pltpu.VMEM((F, R, 2 * A), f32),
            pltpu.VMEM((N, LANES), f32),
            pltpu.VMEM((R, N), f32),
            dma((7 + RC,)),
            dma((C, RC, F)), dma((C, RC, F)),
            dma((C, PC, F)), dma((C, PC, F)),
            dma((PC, CH)), dma((PC, CH)),
            dma((CH,)), dma((CH,)),
            dma((1 + PC,)),
            dma((4,)), dma((4,)),
            dma((PC, CH)), dma((PC, CH)),
            dma((2, PC)),
        ],
        compiler_params=pltpu.CompilerParams(
            collective_id=0, has_side_effects=True, vmem_limit_bytes=60 * 1024 * 1024
        ),
    )(image[0], seed, turn, table, weights, measured, dual)


def solution(mesh):
    placed = (
        P("chan", "facet", None),
        P("chan", None, "facet"),
        P("chan", None, None, "facet"),
        P(None, None, "facet", "chan"),
    )
    return jax.shard_map(
        shards,
        mesh=mesh,
        in_specs=placed,
        out_specs=(P(None, "facet", "chan"), P(None, None, "facet", "chan")),
        check_vma=False,
    )
```

time: 225 us -> 216 us (0.960)
  Pallas kernels: 223 us -> 210 us
  local copies, waits for them, and re-layouts: 0 us -> 4.55 us
    pallas_call x2 -> x1, Pallas kernels: 223 us -> 210 us  [shards(): pl.pallas_call(partial(kernel, F, CH), out_shape=(jax.ShapeDtypeStruct((C...]
    unnamed x0 -> x4, local copies, waits for them, and re-layouts: none -> 4.55 us
where the time goes in v1:
time: 216 us; the launch traced here: 215 us
  Pallas kernels  210 us (97%)
  local copies, waits for them, and re-layouts  4.55 us (2%)
    pallas_call x1, Pallas kernels, shards(): pl.pallas_call(partial(kernel, F, CH), out_shape=(jax.ShapeDtypeStruct((C...  210 us
    unnamed x4, local copies, waits for them, and re-layouts  4.55 us

profile of v1, /device:TPU:9, one launch (start us, length us, event | category | flops | bytes accessed | tf_op | source)
XLA Modules:
  0.0 215.1 jit_solution(14431199469915578838)
XLA Ops:
  0.6 209.9 %shard_map.86 = (f32[4,256,512]{2,1,0:T(8,128)}, bf16[4,2,256,512]{3,2,1,0:T(8,128)(2,1)}) custom-call(f32[256,2048]{1,0:T(8,128)} %bitcast.1, f32[256,512]{1,0:T(8,128)} %constant.6.clone.seed_ref, f32[8,8,512]{2,1,0:T(8,128)} %constant.7.clone.turn_ref, bf16[2,8,256,256]{3,2,1,0:T(8,128)(2,1)} %constant.8.clone.table_hbm, bf16[1,2048,256]{2,1,0:T(8,128)(2,1)} %w_hbm.1, ...), custom_call_target="tpu_custom_call" | custom-call | tf_op jit(solution)/shard_map/pallas_call | solution.py:496
  210.6 0.0 copy-start
  210.6 3.2 %copy.11 = f32[4,256,512]{2,1,0:T(8,128)} copy(f32[4,256,512]{2,1,0:T(8,128)} %get-tuple-element.4) | data formatting | bytes 4194304
  213.8 0.0 copy-done
  213.8 1.3 copy.12
Async XLA Ops:
  210.6 3.2 %copy-start = (bf16[4,2,256,512]{3,2,1,0:T(8,128)(2,1)S(1)}, bf16[4,2,256,512]{3,2,1,0:T(8,128)(2,1)}, u32[]{:S(2)}) copy-start(bf16[4,2,256,512]{3,2,1,0:T(8,128)(2,1)} %get-tuple-element.5) | copy-start | bytes 6291460

commit v2 on v1

--- a/solution.py
+++ b/solution.py
@@ -127,11 +127,11 @@
 
 def kernel(
     F, CH, x_hbm, seed_ref, turn_ref, table_hbm, w_hbm, m_hbm, d_hbm,
-    image_hbm, next_hbm,
-    t_ref, x_ref, image_ref, grad_ref, dual, up, up_ref, low, low_ref,
+    grad_ref, dual,
+    t_ref, x_ref, image_ref, up, up_ref, low, low_ref,
     left, left_ref, right, right_ref, edge, edge_ref, column, parts,
     xt, z, send, recv, wb, mb, wf, mf, u, sendy, recvy, gt, g,
-    in_sem, fs, fr, bs, br, cs, cr, xs, xr, ls, hs, hr, rs, rr, out_sem,
+    in_sem, fs, fr, bs, br, cs, cr, xs, xr, ls, hs, hr, rs, rr,
 ):
     R, N = x_ref.shape
     A = N // F
@@ -387,7 +387,6 @@
                 dual[k, 1, rows, :] = (parts[k, 1] * factor).astype(jnp.bfloat16)
 
     last = [[] for _ in pieces]
-    outs = []
 
     def finish(h):
         start, size = pieces[h]
@@ -414,16 +413,6 @@
         first = max(start // BLOCK - 1, 0)
         end = (start + size) // BLOCK - (0 if final else 1)
         shrink(first, end)
-        done = slice(start, start + size)
-        outs.append(pltpu.make_async_copy(
-            grad_ref.at[:, done, :], image_hbm.at[:, done, :], out_sem.at[0, h]
-        ))
-        done = slice(first * BLOCK, end * BLOCK)
-        outs.append(pltpu.make_async_copy(
-            dual.at[:, :, done, :], next_hbm.at[:, :, done, :], out_sem.at[1, h]
-        ))
-        for copy in outs[-2:]:
-            copy.start()
 
     for h, (start, size) in enumerate(pieces):
         for copy in back[h]:
@@ -472,10 +461,20 @@
         ))
         for copy in last[h]:
             copy.start()
-        if h > 0:
-            finish(h - 1)
-    finish(len(pieces) - 1)
-    for copy in outs:
+        if h >= 2:
+            finish(h - 2)
+    for h in range(max(len(pieces) - 2, 0), len(pieces)):
+        finish(h)
+
+
+def place(image, dual, image_out, dual_out, sem):
+    copies = [
+        pltpu.make_async_copy(image, image_out, sem.at[0]),
+        pltpu.make_async_copy(dual, dual_out, sem.at[1]),
+    ]
+    for copy in copies:
+        copy.start()
+    for copy in copies:
         copy.wait()
 
 
@@ -493,20 +492,19 @@
     dma = pltpu.SemaphoreType.DMA
     vmem = pl.BlockSpec(memory_space=pltpu.VMEM)
     hbm = pl.BlockSpec(memory_space=pl.ANY)
-    return pl.pallas_call(
+    main = pl.BlockSpec(memory_space=pltpu.HBM)
+    staged = pl.pallas_call(
         partial(kernel, F, CH),
         out_shape=(
-            jax.ShapeDtypeStruct((CH, R, T), f32),
-            jax.ShapeDtypeStruct((CH, 2, R, T), jnp.bfloat16),
+            pltpu.VMEM((CH, R, T), f32),
+            pltpu.VMEM((CH, 2, R, T), jnp.bfloat16),
         ),
-        in_specs=[hbm, vmem, vmem, hbm, hbm, hbm, hbm],
-        out_specs=(hbm, hbm),
+        in_specs=[main, vmem, vmem, main, main, main, main],
+        out_specs=(vmem, vmem),
         scratch_shapes=[
             pltpu.VMEM((2, F, A, 2 * A), jnp.bfloat16),
             pltpu.VMEM((R, N), f32),
             pltpu.VMEM((CH, R + 8, T), f32),
-            pltpu.VMEM((CH, R, T), f32),
-            pltpu.VMEM((CH, 2, R, T), jnp.bfloat16),
             pltpu.VMEM((HR, T), f32),
             pltpu.VMEM((HR, T), f32),
             pltpu.VMEM((HR, T), f32),
@@ -540,12 +538,19 @@
             dma((1 + PC,)),
             dma((4,)), dma((4,)),
             dma((PC, CH)), dma((PC, CH)),
-            dma((2, PC)),
         ],
         compiler_params=pltpu.CompilerParams(
-            collective_id=0, has_side_effects=True, vmem_limit_bytes=60 * 1024 * 1024
+            collective_id=0, has_side_effects=True, vmem_limit_bytes=54 * 1024 * 1024
         ),
     )(image[0], seed, turn, table, weights, measured, dual)
+    return pl.pallas_call(
+        place,
+        out_shape=tuple(jax.ShapeDtypeStruct(a.shape, a.dtype) for a in staged),
+        in_specs=[hbm, hbm],
+        out_specs=(hbm, hbm),
+        scratch_shapes=[dma((2,))],
+        compiler_params=pltpu.CompilerParams(vmem_limit_bytes=2 * 1024 * 1024),
+    )(*staged)
 
 
 def solution(mesh):

time: 216 us -> 207 us (0.958)
  local copies, waits for them, and re-layouts: 4.55 us -> 0 us
  Pallas kernels: 210 us -> 207 us
    unnamed x4 -> x0, local copies, waits for them, and re-layouts: 4.55 us -> none
    pallas_call x1 -> x2, Pallas kernels: 210 us -> 207 us  [the longest x1 205 us: shards(): pl.pallas_call(partial(kernel, F, CH), out_shape=(pltpu.VMEM((CH, R, T),...]
where the time goes in v2:
time: 207 us
  Pallas kernels  207 us (100%)
    pallas_call x1, Pallas kernels, shards(): pl.pallas_call(partial(kernel, F, CH), out_shape=(pltpu.VMEM((CH, R, T),...  205 us

profile of v2, /device:TPU:9, one launch (start us, length us, event | category | flops | bytes accessed | tf_op | source)
XLA Modules:
  0.0 207.2 jit_solution(1936254381511269062)
XLA Ops:
  0.6 204.6 %shard_map.86 = (f32[4,256,512]{2,1,0:T(8,128)S(1)}, bf16[4,2,256,512]{3,2,1,0:T(8,128)(2,1)S(1)}) custom-call(f32[256,2048]{1,0:T(8,128)} %bitcast.1, f32[256,512]{1,0:T(8,128)} %constant.6.clone.seed_ref, f32[8,8,512]{2,1,0:T(8,128)} %constant.7.clone.turn_ref, bf16[2,8,256,256]{3,2,1,0:T(8,128)(2,1)} %constant.8.clone.table_hbm, ...), custom_call_target="tpu_custom_call" | custom-call | tf_op jit(solution)/shard_map/pallas_call | solution.py:496
  205.2 2.0 shard_map.87

commit v3 on v2

--- a/solution.py
+++ b/solution.py
@@ -101,10 +101,11 @@
 
 def back_pieces(rows):
     pieces, start = [], 0
-    for part in (4, 4, 4, 8, 8):
-        pieces.append((start, rows // part))
-        start += rows // part
-    return pieces
+    while rows - start > 2 * BLOCK:
+        size = (rows - start) // 2
+        pieces.append((start, size))
+        start += size
+    return pieces + [(start, rows - start)]
 
 
 def square_tables(t_ref, k, chunks):
@@ -300,28 +301,30 @@
             u[k, :, 0:LANES] = p[:, 0:LANES] + q[:, LANES:]
             u[k, :, LANES:W] = p[:, LANES:] - q[:, 0:LANES]
 
-        for i, (start, size) in enumerate(pieces if c == C - 1 else [(0, R)]):
-
-            @pl.loop(0, size // 8)
-            def _(t):
-                rows = pl.ds(pl.multiple_of(start + t * 8, 8), 8)
-                values = [(u[k, rows, 0:LANES], u[k, rows, LANES:W]) for k in range(F)]
-                for q, (re, im) in enumerate(block_dft(values, 1.0)):
-                    sendy[q, rows, c * W:c * W + LANES] = re
-                    sendy[q, rows, c * W + LANES:(c + 1) * W] = im
-
+        @pl.loop(0, R // 8)
+        def _(t):
+            rows = pl.ds(pl.multiple_of(t * 8, 8), 8)
+            values = [(u[k, rows, 0:LANES], u[k, rows, LANES:W]) for k in range(F)]
+            for q, (re, im) in enumerate(block_dft(values, 1.0)):
+                sendy[q, rows, c * W:c * W + LANES] = re
+                sendy[q, rows, c * W + LANES:(c + 1) * W] = im
+
+        parcels = [(0, pieces[0], wide)]
+        if c == C - 1:
+            parcels += [(i, piece, slice(0, C * W)) for i, piece in enumerate(pieces) if i > 0]
+        for i, (start, size), across in parcels:
             span = pl.ds(start, size)
             for o in order:
                 d = lax.rem(me + o, F)
                 copy = pltpu.make_async_remote_copy(
-                    src_ref=sendy.at[d, span, wide], dst_ref=recvy.at[me, span, wide],
+                    src_ref=sendy.at[d, span, across], dst_ref=recvy.at[me, span, across],
                     send_sem=bs.at[c, i, o], recv_sem=br.at[c, i, o],
                     device_id={"facet": d}, device_id_type=pl.DeviceIdType.MESH,
                 )
                 copy.start()
                 back[i].append(copy)
             copy = pltpu.make_async_copy(
-                sendy.at[me, span, wide], recvy.at[me, span, wide], br.at[c, i, 0]
+                sendy.at[me, span, across], recvy.at[me, span, across], br.at[c, i, 0]
             )
             copy.start()
             back[i].append(copy)
@@ -431,7 +434,7 @@
 
         span = pl.ds(start, size)
 
-        @pl.loop(0, F)
+        @pl.loop(0, F, unroll=F)
         def _(b):
             line = exact_dot((t_ref[0, b], t_ref[1, b]), halves(z[b]), ((1,), (1,)))
             gt[pl.ds(b, A, stride=F), :] = line * scale

time: 207 us -> 202 us (0.976)
  Pallas kernels: 207 us -> 201 us
    pallas_call x1, Pallas kernels: 205 us -> 199 us  [shards(): pl.pallas_call(partial(kernel, F, CH), out_shape=(pltpu.VMEM((CH, R, T),...]
where the time goes in v3:
time: 202 us
  Pallas kernels  201 us (100%)
    pallas_call x1, Pallas kernels, shards(): pl.pallas_call(partial(kernel, F, CH), out_shape=(pltpu.VMEM((CH, R, T),...  199 us

profile of v3, /device:TPU:9, one launch (start us, length us, event | category | flops | bytes accessed | tf_op | source)
XLA Modules:
  0.0 201.6 jit_solution(4518836582157620860)
XLA Ops:
  0.6 198.9 %shard_map.86 = (f32[4,256,512]{2,1,0:T(8,128)S(1)}, bf16[4,2,256,512]{3,2,1,0:T(8,128)(2,1)S(1)}) custom-call(f32[256,2048]{1,0:T(8,128)} %bitcast.1, f32[256,512]{1,0:T(8,128)} %constant.6.clone.seed_ref, f32[8,8,512]{2,1,0:T(8,128)} %constant.7.clone.turn_ref, bf16[2,8,256,256]{3,2,1,0:T(8,128)(2,1)} %constant.8.clone.table_hbm, ...), custom_call_target="tpu_custom_call" | custom-call | tf_op jit(solution)/shard_map/pallas_call | solution.py:499
  199.6 2.0 %shard_map.87 = (f32[4,256,512]{2,1,0:T(8,128)}, bf16[4,2,256,512]{3,2,1,0:T(8,128)(2,1)}) custom-call(f32[4,256,512]{2,1,0:T(8,128)S(1)} %get-tuple-element.4.image, bf16[4,2,256,512]{3,2,1,0:T(8,128)(2,1)S(1)} %get-tuple-element.5.dual), custom_call_target="tpu_custom_call" | custom-call | tf_op jit(solution)/shard_map/pallas_call | solution.py:549

commit v4 on v3

--- a/solution.py
+++ b/solution.py
@@ -348,7 +348,7 @@
     lane = lax.broadcasted_iota(jnp.int32, (BLOCK, T), 1)
 
     def primal(first, end):
-        @pl.loop(first, end)
+        @pl.loop(first, end, unroll=(end - first) if end - first < 4 else 1)
         def _(at):
             rows = pl.ds(pl.multiple_of(at * BLOCK, BLOCK), BLOCK)
             ahead = pl.ds(pl.multiple_of(jnp.maximum(at - 1, 0) * BLOCK, BLOCK), BLOCK)
@@ -367,7 +367,7 @@
                 image_ref[k, rows, :] = 2.0 * value - x
 
     def shrink(first, end):
-        @pl.loop(first, end)
+        @pl.loop(first, end, unroll=(end - first) if end - first < 4 else 1)
         def _(at):
             rows = pl.ds(pl.multiple_of(at * BLOCK, BLOCK), BLOCK)
             later = pl.ds(pl.multiple_of(at * BLOCK + BLOCK, BLOCK), 8)

time: 202 us -> 201 us (level)
  no operation moved by 1% of the time
where the time goes in v4:
time: 201 us
  Pallas kernels  201 us (100%)
    pallas_call x1, Pallas kernels, shards(): pl.pallas_call(partial(kernel, F, CH), out_shape=(pltpu.VMEM((CH, R, T),...  199 us

profile of v4, /device:TPU:9, one launch (start us, length us, event | category | flops | bytes accessed | tf_op | source)
XLA Modules:
  0.0 201.3 jit_solution(2677256914594102778)
XLA Ops:
  0.6 198.6 %shard_map.86 = (f32[4,256,512]{2,1,0:T(8,128)S(1)}, bf16[4,2,256,512]{3,2,1,0:T(8,128)(2,1)S(1)}) custom-call(f32[256,2048]{1,0:T(8,128)} %bitcast.1, f32[256,512]{1,0:T(8,128)} %constant.6.clone.seed_ref, f32[8,8,512]{2,1,0:T(8,128)} %constant.7.clone.turn_ref, bf16[2,8,256,256]{3,2,1,0:T(8,128)(2,1)} %constant.8.clone.table_hbm, ...), custom_call_target="tpu_custom_call" | custom-call | tf_op jit(solution)/shard_map/pallas_call | solution.py:499
  199.3 2.0 %shard_map.87 = (f32[4,256,512]{2,1,0:T(8,128)}, bf16[4,2,256,512]{3,2,1,0:T(8,128)(2,1)}) custom-call(f32[4,256,512]{2,1,0:T(8,128)S(1)} %get-tuple-element.4.image, bf16[4,2,256,512]{3,2,1,0:T(8,128)(2,1)S(1)} %get-tuple-element.5.dual), custom_call_target="tpu_custom_call" | custom-call | tf_op jit(solution)/shard_map/pallas_call | solution.py:549

commit v5 on v4

--- a/solution.py
+++ b/solution.py
@@ -471,10 +471,12 @@
 
 
 def place(image, dual, image_out, dual_out, sem):
-    copies = [
-        pltpu.make_async_copy(image, image_out, sem.at[0]),
-        pltpu.make_async_copy(dual, dual_out, sem.at[1]),
-    ]
+    copies = []
+    for k in range(image.shape[0]):
+        copies += [
+            pltpu.make_async_copy(image.at[k], image_out.at[k], sem.at[0, k]),
+            pltpu.make_async_copy(dual.at[k], dual_out.at[k], sem.at[1, k]),
+        ]
     for copy in copies:
         copy.start()
     for copy in copies:
@@ -551,7 +553,7 @@
         out_shape=tuple(jax.ShapeDtypeStruct(a.shape, a.dtype) for a in staged),
         in_specs=[hbm, hbm],
         out_specs=(hbm, hbm),
-        scratch_shapes=[dma((2,))],
+        scratch_shapes=[dma((2, CH))],
         compiler_params=pltpu.CompilerParams(vmem_limit_bytes=2 * 1024 * 1024),
     )(*staged)
 

time: 201 us -> 201 us (level)
  no operation moved by 1% of the time
where the time goes in v5:
time: 201 us
  Pallas kernels  201 us (100%)
    pallas_call x1, Pallas kernels, shards(): pl.pallas_call(partial(kernel, F, CH), out_shape=(pltpu.VMEM((CH, R, T),...  199 us

profile of v5, /device:TPU:9, one launch (start us, length us, event | category | flops | bytes accessed | tf_op | source)
XLA Modules:
  0.0 201.3 jit_solution(12778176946853133938)
XLA Ops:
  0.6 198.6 %shard_map.86 = (f32[4,256,512]{2,1,0:T(8,128)S(1)}, bf16[4,2,256,512]{3,2,1,0:T(8,128)(2,1)S(1)}) custom-call(f32[256,2048]{1,0:T(8,128)} %bitcast.1, f32[256,512]{1,0:T(8,128)} %constant.6.clone.seed_ref, f32[8,8,512]{2,1,0:T(8,128)} %constant.7.clone.turn_ref, bf16[2,8,256,256]{3,2,1,0:T(8,128)(2,1)} %constant.8.clone.table_hbm, ...), custom_call_target="tpu_custom_call" | custom-call | tf_op jit(solution)/shard_map/pallas_call | solution.py:501
  199.3 2.1 %shard_map.87 = (f32[4,256,512]{2,1,0:T(8,128)}, bf16[4,2,256,512]{3,2,1,0:T(8,128)(2,1)}) custom-call(f32[4,256,512]{2,1,0:T(8,128)S(1)} %get-tuple-element.4.image, bf16[4,2,256,512]{3,2,1,0:T(8,128)(2,1)S(1)} %get-tuple-element.5.dual), custom_call_target="tpu_custom_call" | custom-call | tf_op jit(solution)/shard_map/pallas_call | solution.py:551

commit v6 on v5

--- a/solution.py
+++ b/solution.py
@@ -464,9 +464,9 @@
         ))
         for copy in last[h]:
             copy.start()
-        if h >= 2:
-            finish(h - 2)
-    for h in range(max(len(pieces) - 2, 0), len(pieces)):
+        if h >= 3:
+            finish(h - 3)
+    for h in range(max(len(pieces) - 3, 0), len(pieces)):
         finish(h)
 
 

time: 201 us -> 201 us (level)
  no operation moved by 1% of the time
where the time goes in v6:
time: 201 us
  Pallas kernels  201 us (100%)
    pallas_call x1, Pallas kernels, shards(): pl.pallas_call(partial(kernel, F, CH), out_shape=(pltpu.VMEM((CH, R, T),...  199 us

profile of v6, /device:TPU:9, one launch (start us, length us, event | category | flops | bytes accessed | tf_op | source)
XLA Modules:
  0.0 201.3 jit_solution(12820826566385702087)
XLA Ops:
  0.6 198.6 %shard_map.86 = (f32[4,256,512]{2,1,0:T(8,128)S(1)}, bf16[4,2,256,512]{3,2,1,0:T(8,128)(2,1)S(1)}) custom-call(f32[256,2048]{1,0:T(8,128)} %bitcast.1, f32[256,512]{1,0:T(8,128)} %constant.6.clone.seed_ref, f32[8,8,512]{2,1,0:T(8,128)} %constant.7.clone.turn_ref, bf16[2,8,256,256]{3,2,1,0:T(8,128)(2,1)} %constant.8.clone.table_hbm, ...), custom_call_target="tpu_custom_call" | custom-call | tf_op jit(solution)/shard_map/pallas_call | solution.py:501
  199.3 2.1 %shard_map.87 = (f32[4,256,512]{2,1,0:T(8,128)}, bf16[4,2,256,512]{3,2,1,0:T(8,128)(2,1)}) custom-call(f32[4,256,512]{2,1,0:T(8,128)S(1)} %get-tuple-element.4.image, bf16[4,2,256,512]{3,2,1,0:T(8,128)(2,1)S(1)} %get-tuple-element.5.dual), custom_call_target="tpu_custom_call" | custom-call | tf_op jit(solution)/shard_map/pallas_call | solution.py:551
